TPU v7x, 256 devices: a whole 4x4x8 slice. The times are simulated.
256 devices in a mesh: seq: 32 (over x, y, core), dp: 8 (over z).
Axes of the slice: x: 4, y: 4, z: 8, core: 2. Of those that a mesh axis runs over, the one named last changes fastest.
Arguments:
- points: bfloat16 [8, 16384, 512], P('dp', 'seq'), may hold values from -6 to 6
- cotangent: bfloat16 [8, 16384, 512], P('dp', 'seq'), may hold values from -6 to 6
- dest: int32 [8, 16384], P('dp', 'seq'), may hold values from 0 to 16383, as said below
- w_qkv: bfloat16 [512, 1536], replicated
- w_proj: bfloat16 [512, 512], replicated, may hold values from -0.25 to 0.25
- gain: float32 [512], replicated, may hold values from 0.5 to 1.5
Outputs:
- grad_points: bfloat16 [8, 16384, 512], P('dp', 'seq')
- grad_qkv: float32 [512, 1536], replicated
- grad_proj: float32 [512, 512], replicated
- gain_gradient: float32 [512], replicated
Inputs may be any that keep to these rules, and one draw needn't show every extreme that they name: For each scan, dest is a permutation of the 16384 positions, one serialization order of the points. Of the 512 points of one device, at most 32 have positions on any one device's range of 512 positions, and exactly 32 for some device.
All inputs are finite; a program needn't handle non-finite values.
Results may differ from a plain program's by a relative error of at most 0.013.
The roundings to bfloat16 on the way count: a program that leaves them out, or rounds other values in their place, can miss the bound.
Values may be sent and summed in bfloat16 or wider, within the bound.
A program may use at most 64 MiB of HBM per device.

v0:
```python
import jax
import jax.numpy as jnp
from jax import lax
from jax.sharding import Mesh
from jax.sharding import PartitionSpec as P

HEADS = 8
PATCH = 512
SEQ = ("seq_0", "seq_1", "seq_2")
SEQ_DP = ("seq_0", "seq_1", "seq_2", "dp")


def split_up(shard, dim, length):
    before, after = (shard.shape[:dim], shard.shape[dim + 1 :])
    return jnp.moveaxis(shard.reshape(*before, length, -1, *after), dim, 0)


def laid_out(parts, dim):
    shape = list(parts.shape[1:])
    shape[dim] *= parts.shape[0]
    return jnp.moveaxis(parts, 0, dim).reshape(shape)


def turned_blocks(parts, axes, sequence):
    shape = [lax.axis_size(a) for a in axes]
    parts = parts.reshape(*shape, *parts.shape[1:])
    for k in sequence:
        parts = lax.all_to_all(parts, axes[k], split_axis=k, concat_axis=k, tiled=True)
    return parts.reshape(-1, *parts.shape[len(axes) :])


def two_step_exchange(shard, groups, sequence, split_dim, concat_dim):
    length = lax.axis_size(groups[0]) * lax.axis_size(groups[1])
    parts = split_up(shard, split_dim, length)
    return laid_out(turned_blocks(parts, groups, sequence), concat_dim)


def per_device(points, cotangent, dest, w_qkv, w_proj, gain):
    feats_in = points[0]
    grads_in = cotangent[0]
    places = dest[0]
    rows_dev = feats_in.shape[0]
    width = feats_in.shape[1]
    n_seq = lax.axis_size(SEQ)
    capacity = 2 * (rows_dev // n_seq)
    owner = places // rows_dev
    slot_local = places % rows_dev
    onehot = (owner[:, None] == jnp.arange(n_seq, dtype=jnp.int32)[None, :]).astype(jnp.int32)
    rank = jnp.sum((jnp.cumsum(onehot, axis=0) - 1) * onehot, axis=1)
    send_slot = owner * capacity + rank
    send_pos = jnp.full((n_seq * capacity,), rows_dev, jnp.int32).at[send_slot].set(slot_local)
    send_pos = send_pos.reshape(n_seq, capacity)

    def pack(values):
        filled = jnp.zeros((n_seq * capacity, width), values.dtype).at[send_slot].set(values)
        return filled.reshape(n_seq, capacity, width)

    def unpack(received, recv_flat):
        flat_vals = received.reshape(n_seq * capacity, width)
        return (
            jnp.zeros((rows_dev, width), received.dtype).at[recv_flat].set(flat_vals, mode="drop")
        )

    recv_feats, recv_pos = (
        two_step_exchange(pack(feats_in), (("seq_0", "seq_1"), "seq_2"), (0, 1), 0, 0),
        two_step_exchange(send_pos, (("seq_0", "seq_1"), "seq_2"), (0, 1), 0, 0),
    )
    recv_flat = recv_pos.reshape(-1)
    serial = unpack(recv_feats, recv_flat)
    feats = serial.astype(jnp.float32)
    centered_input = feats - jnp.mean(feats, axis=1, keepdims=True)
    inverse_deviation = lax.rsqrt(
        jnp.mean(centered_input * centered_input, axis=1, keepdims=True) + 1e-05
    )
    standardized_input = centered_input * inverse_deviation
    normalized_input = (standardized_input * gain[None, :]).astype(jnp.bfloat16)
    qkv = jnp.dot(normalized_input, w_qkv, preferred_element_type=jnp.float32).astype(jnp.bfloat16)
    recv_grads = lax.all_to_all(pack(grads_in), SEQ, split_axis=0, concat_axis=0, tiled=True)
    serial_grad = unpack(recv_grads, recv_flat)
    d_attn = jnp.dot(serial_grad, w_proj.T, preferred_element_type=jnp.float32).astype(jnp.bfloat16)
    patches = rows_dev // PATCH
    head_dim = width // HEADS
    group_heads = 2
    group_cols = group_heads * head_dim
    scale = 1.0 / head_dim**0.5
    attn_list, dq_list, dk_list, dv_list = ([], [], [], [])
    for group_idx in range(HEADS // group_heads):
        lo_col = group_idx * group_cols
        shape_four = (patches, PATCH, group_heads, head_dim)
        query = qkv[:, lo_col : lo_col + group_cols].reshape(shape_four)
        keys = qkv[:, width + lo_col : width + lo_col + group_cols].reshape(shape_four)
        values = qkv[:, 2 * width + lo_col : 2 * width + lo_col + group_cols].reshape(shape_four)
        grad_head = d_attn[:, lo_col : lo_col + group_cols].reshape(shape_four)
        scores = (
            jnp.einsum("pqhd,pkhd->phqk", query, keys, preferred_element_type=jnp.float32) * scale
        )
        top = jnp.max(scores, axis=3, keepdims=True)
        expo = jnp.exp(scores - top)
        probs = expo / jnp.sum(expo, axis=3, keepdims=True)
        probs_b = probs.astype(jnp.bfloat16)
        attn_list.append(
            jnp.einsum("phqk,pkhd->pqhd", probs_b, values, preferred_element_type=jnp.float32)
            .astype(jnp.bfloat16)
            .reshape(rows_dev, group_cols)
        )
        d_probs = jnp.einsum(
            "pqhd,pkhd->phqk", grad_head, values, preferred_element_type=jnp.float32
        )
        d_scores = (
            probs * (d_probs - jnp.sum(d_probs * probs, axis=3, keepdims=True)) * scale
        ).astype(jnp.bfloat16)
        dq_list.append(
            jnp.einsum("phqk,pkhd->pqhd", d_scores, keys, preferred_element_type=jnp.float32)
            .astype(jnp.bfloat16)
            .reshape(rows_dev, group_cols)
        )
        dk_list.append(
            jnp.einsum("phqk,pqhd->pkhd", d_scores, query, preferred_element_type=jnp.float32)
            .astype(jnp.bfloat16)
            .reshape(rows_dev, group_cols)
        )
        dv_list.append(
            jnp.einsum("phqk,pqhd->pkhd", probs_b, grad_head, preferred_element_type=jnp.float32)
            .astype(jnp.bfloat16)
            .reshape(rows_dev, group_cols)
        )
    attn = jnp.concatenate(attn_list, axis=1)
    d_qkv = jnp.concatenate(dq_list + dk_list + dv_list, axis=1)
    grad_proj = jnp.einsum("rc,rd->cd", attn, serial_grad, preferred_element_type=jnp.float32)
    grad_qkv = jnp.einsum("rc,rd->cd", normalized_input, d_qkv, preferred_element_type=jnp.float32)
    normalized_gradient = jnp.dot(d_qkv, w_qkv.T, preferred_element_type=jnp.float32)
    gain_gradient = jnp.sum(normalized_gradient * standardized_input, axis=0)
    gain_scaled = normalized_gradient * gain[None, :]
    residual_branch = inverse_deviation * (
        gain_scaled
        - jnp.mean(gain_scaled, axis=1, keepdims=True)
        - standardized_input * jnp.mean(gain_scaled * standardized_input, axis=1, keepdims=True)
    )
    serial_dx = (serial_grad.astype(jnp.float32) + residual_branch).astype(jnp.bfloat16)
    back_rows = serial_dx[jnp.minimum(recv_flat, rows_dev - 1)].reshape(n_seq, capacity, width)
    returned = lax.all_to_all(back_rows, SEQ, split_axis=0, concat_axis=0, tiled=True)
    grad_local = returned.reshape(n_seq * capacity, width)[send_slot]
    grad_qkv, grad_proj, gain_gradient = lax.psum((grad_qkv, grad_proj, gain_gradient), SEQ_DP)
    return (grad_local[None], grad_qkv, grad_proj, gain_gradient)


def solution(mesh):
    finer = Mesh(mesh.devices.reshape(4, 4, 2, mesh.shape["dp"]), ("seq_0", "seq_1", "seq_2", "dp"))
    placed = (P("dp", SEQ, None), P("dp", SEQ, None), P("dp", SEQ), P(), P(), P())
    return jax.shard_map(
        per_device,
        mesh=finer,
        in_specs=placed,
        out_specs=(P("dp", SEQ, None), P(), P(), P()),
        check_vma=False,
    )
```

profile of v0, /device:TPU:1, one launch (start us, length us, event | category | flops | bytes accessed | tf_op | source)
XLA Modules:
  0.0 454.0 jit_solution(13104250691311163556)
XLA Ops:
  7.2 0.8 add_select_fusion.1
  8.0 0.7 add_select_fusion
  8.7 1.2 reduce-window.6
  10.2 0.7 compare_select_fusion.2
  10.9 2.4 scatter_custom_fusion
  13.4 0.7 reshape_reshape_reshape.12
  14.1 7.6 %all-to-all-start = ((s32[16,2,1,32]{3,1,2,0:T(2,128)}), s32[16,2,1,32]{3,1,2,0:T(2,128)S(1)}, u32[]{:S(2)}, u32[]{:S(2)}) async-start(s32[16,2,1,32]{3,1,2,0:T(2,128)} %bitcast.6), calls=%async_computation | async-start | bytes 32768 | tf_op jit(solution)/shard_map/all_to_all | solution.py:28
  21.7 4.0 scatter_custom_fusion.3
  25.6 2.5 all-to-all-done
  28.7 0.7 reduce.26
  29.4 5.5 %all_to_all.30 = s32[2,1,512]{2,1,0:T(1,128)S(1)} all-to-all(s32[2,1,512]{2,1,0:T(1,128)S(1)} %reshape.644), channel_id=1, replica_groups=mesh['seq_0'=4,'seq_1'=4,'seq_2'=2,'dp'=8] {'seq_2'}, dimensions={0} | all-to-all | bytes 8192 | tf_op jit(solution)/shard_map/all_to_all | solution.py:28
  34.9 3.7 all-to-all-start.3
  38.6 3.5 scatter_custom_fusion.1
  42.9 12.2 %all-to-all-done.3 = bf16[16,2,1,32,512]{4,3,1,2,0:T(8,128)(2,1)S(1)} async-done(((bf16[16,2,1,32,512]{4,3,1,2,0:T(8,128)(2,1)}), bf16[16,2,1,32,512]{4,3,1,2,0:T(8,128)(2,1)S(1)}, u32[]{:S(2)}, u32[]{:S(2)}) %all-to-all-start.3) | async-done | bytes 1048608 | tf_op jit(solution)/shard_map/all_to_all | solution.py:28
  55.2 6.4 %all_to_all.31 = bf16[16,2,1,32,512]{4,3,0,2,1:T(8,128)(2,1)S(1)} all-to-all(bf16[16,2,1,32,512]{4,3,0,2,1:T(8,128)(2,1)S(1)} %copy.161), channel_id=1, replica_groups=mesh['seq_0'=4,'seq_1'=4,'seq_2'=2,'dp'=8] {'seq_2'}, dimensions={1} | all-to-all | bytes 2097152 | tf_op jit(solution)/shard_map/all_to_all | solution.py:28
  61.6 4.6 %all-to-all-start.2 = ((bf16[32,32,512]{2,1,0:T(8,128)(2,1)}), bf16[32,32,512]{2,1,0:T(8,128)(2,1)}, u32[]{:S(2)}, u32[]{:S(2)}) async-start(bf16[32,32,512]{2,1,0:T(8,128)(2,1)} %bitcast.9), calls=%async_computation.2 | async-start | bytes 2097152 | tf_op jit(solution)/shard_map/all_to_all | solution.py:78
  66.2 1.0 copy.162
  67.3 6.1 %scatter_custom_fusion.4 = bf16[512,512]{1,0:T(8,128)(2,1)S(1)} fusion(s32[1024]{0:T(1024)S(1)} %bitcast.283, bf16[1024,512]{1,0:T(8,128)(2,1)} %bitcast.211, bf16[]{:T(256)} %constant.46.clone.1), kind=kCustom, calls=%fused_computation.120 | custom fusion | bytes 524800 | tf_op jit(solution)/shard_map/scatter | solution.py:61
  73.9 1.1 convolution_convert_fusion
  75.0 1.0 fusion.196
  76.1 0.8 copy.177
  76.8 1.0 copy.178
  77.8 0.8 copy.176
  78.7 0.8 copy.173
  80.4 2.2 fusion.198
  82.6 1.8 convolution_convert_fusion.5
  84.4 2.2 fusion.199
  86.6 1.8 convolution_convert_fusion.4
  88.4 2.2 fusion.200
  90.5 1.8 convolution_convert_fusion.3
  92.3 2.2 fusion.201
  94.5 1.8 convolution_convert_fusion.2
  96.3 5.8 %scatter_custom_fusion.2 = bf16[512,512]{1,0:T(8,128)(2,1)S(1)} fusion(s32[1024]{0:T(1024)} %bitcast.284, bf16[1024,512]{1,0:T(8,128)(2,1)} %bitcast.10, bf16[]{:T(256)} %constant.46.clone.1), kind=kCustom, calls=%fused_computation.122 | custom fusion | bytes 524800 | tf_op jit(solution)/shard_map/scatter | solution.py:61
  103.0 1.8 fusion.202
  104.8 2.8 convolution_convert_fusion.9
  107.6 5.0 %fusion.75 = bf16[2,64,512]{2,1,0:T(8,128)(2,1)} fusion(bf16[512,2,64]{0,2,1:T(8,128)(2,1)} %bitcast.261, f32[2,512,512]{1,2,0:T(8,128)} %fusion.202, f32[2,512,512]{1,2,0:T(8,128)} %get-tuple-element.30, f32[2,512]{1,0:T(2,128)} %copy-done.39), kind=kOutput, calls=%fused_computation.64 | convolution fusion | flops 70845952 | bytes 4460544 | tf_op jit(solution)/shard_map/phqk,pqhd->pkhd/dot_general | solution.py:118
  112.6 5.1 %fusion.72 = bf16[2,64,512]{2,1,0:T(8,128)(2,1)} fusion(bf16[512,2,64]{0,2,1:T(8,128)(2,1)S(1)} %bitcast.267, f32[2,512,512]{1,2,0:T(8,128)} %fusion.202, f32[2,512,512]{1,2,0:T(8,128)} %get-tuple-element.30, f32[2,512]{1,0:T(2,128)} %copy-done.39), kind=kOutput, calls=%fused_computation.63 | convolution fusion | flops 70845952 | bytes 4460544 | tf_op jit(solution)/shard_map/phqk,pkhd->pqhd/dot_general | solution.py:113
  117.7 1.8 fusion.203
  119.5 2.1 convolution_convert_fusion.8
  121.6 5.0 %fusion.69 = bf16[2,64,512]{2,1,0:T(8,128)(2,1)} fusion(bf16[512,2,64]{0,2,1:T(8,128)(2,1)S(1)} %bitcast.250, f32[2,512,512]{1,2,0:T(8,128)} %fusion.203, f32[2,512,512]{1,2,0:T(8,128)} %get-tuple-element.32, f32[2,512]{1,0:T(2,128)} %copy-done.38), kind=kOutput, calls=%fused_computation.62 | convolution fusion | flops 70845952 | bytes 4460544 | tf_op jit(solution)/shard_map/phqk,pqhd->pkhd/dot_general | solution.py:118
  126.6 5.2 %fusion.66 = bf16[2,64,512]{2,1,0:T(8,128)(2,1)} fusion(bf16[512,2,64]{0,2,1:T(8,128)(2,1)S(1)} %bitcast.254, f32[2,512,512]{1,2,0:T(8,128)} %fusion.203, f32[2,512,512]{1,2,0:T(8,128)} %get-tuple-element.32, f32[2,512]{1,0:T(2,128)} %copy-done.38), kind=kOutput, calls=%fused_computation.61 | convolution fusion | flops 70845952 | bytes 4460544 | tf_op jit(solution)/shard_map/phqk,pkhd->pqhd/dot_general | solution.py:113
  131.8 1.8 fusion.204
  133.6 1.8 convolution_convert_fusion.7
  135.5 4.9 %fusion.63 = bf16[2,64,512]{2,1,0:T(8,128)(2,1)} fusion(bf16[512,2,64]{0,2,1:T(8,128)(2,1)S(1)} %bitcast.240, f32[2,512,512]{1,2,0:T(8,128)} %fusion.204, f32[2,512,512]{1,2,0:T(8,128)} %get-tuple-element.34, f32[2,512]{1,0:T(2,128)} %copy-done.36), kind=kOutput, calls=%fused_computation.60 | convolution fusion | flops 70845952 | bytes 4460544 | tf_op jit(solution)/shard_map/phqk,pqhd->pkhd/dot_general | solution.py:118
  140.4 5.1 %fusion.60 = bf16[2,64,512]{2,1,0:T(8,128)(2,1)} fusion(bf16[512,2,64]{0,2,1:T(8,128)(2,1)S(1)} %bitcast.244, f32[2,512,512]{1,2,0:T(8,128)} %fusion.204, f32[2,512,512]{1,2,0:T(8,128)} %get-tuple-element.34, f32[2,512]{1,0:T(2,128)S(1)} %copy-done.37), kind=kOutput, calls=%fused_computation.59 | convolution fusion | flops 70845952 | bytes 4460544 | tf_op jit(solution)/shard_map/phqk,pkhd->pqhd/dot_general | solution.py:113
  145.5 1.8 fusion.205
  147.3 1.2 convolution_convert_fusion.6
  148.5 5.0 %fusion.57 = bf16[2,64,512]{2,1,0:T(8,128)(2,1)} fusion(bf16[512,2,64]{0,2,1:T(8,128)(2,1)S(1)} %bitcast.232, f32[2,512,512]{1,2,0:T(8,128)} %fusion.205, f32[2,512,512]{1,2,0:T(8,128)} %get-tuple-element.36, f32[2,512]{1,0:T(2,128)S(1)} %copy-done.35), kind=kOutput, calls=%fused_computation.58 | convolution fusion | flops 70845952 | bytes 4460544 | tf_op jit(solution)/shard_map/phqk,pqhd->pkhd/dot_general | solution.py:118
  153.5 5.1 %fusion.54 = bf16[2,64,512]{2,1,0:T(8,128)(2,1)} fusion(bf16[512,2,64]{0,2,1:T(8,128)(2,1)S(1)} %bitcast.236, f32[2,512,512]{1,2,0:T(8,128)} %fusion.205, f32[2,512,512]{1,2,0:T(8,128)} %get-tuple-element.36, f32[2,512]{1,0:T(2,128)} %copy-done.34), kind=kOutput, calls=%fused_computation.57 | convolution fusion | flops 70845952 | bytes 4460544 | tf_op jit(solution)/shard_map/phqk,pkhd->pqhd/dot_general | solution.py:113
  158.6 1.0 constant_dynamic-update-slice_fusion.10
  159.6 0.9 constant_dynamic-update-slice_fusion.9
  160.5 0.9 constant_dynamic-update-slice_fusion.8
  161.5 0.9 constant_dynamic-update-slice_fusion.5
  162.4 0.9 constant_dynamic-update-slice_fusion.4
  163.7 2.7 fusion.132
  166.4 1.4 fusion.98
  168.5 2.6 fusion.84
  171.8 5.1 %gather_fusion = bf16[1024,512]{1,0:T(8,128)(2,1)} fusion(bf16[512,512]{1,0:T(8,128)(2,1)S(1)} %copy.188, s32[1024]{0:T(1024)S(1)} %broadcast_clamp_fusion), kind=kCustom, calls=%fused_computation | custom fusion | bytes 2101248 | tf_op jit(solution)/shard_map/gather | solution.py:140
  176.8 7.5 %all-to-all-start.5 = ((bf16[32,32,512]{2,1,0:T(8,128)(2,1)}), bf16[32,32,512]{2,1,0:T(8,128)(2,1)S(1)}, u32[]{:S(2)}, u32[]{:S(2)}) async-start(bf16[32,32,512]{2,1,0:T(8,128)(2,1)} %bitcast.210), calls=%async_computation.5 | async-start | bytes 2097152 | tf_op jit(solution)/shard_map/all_to_all | solution.py:141
  184.4 85.8 %psum.23 = f32[512]{0:T(512)} all-reduce(f32[512]{0:T(512)S(1)} %get-tuple-element.4), channel_id=1, replica_groups=mesh['seq_0'=4,'seq_1'=4,'seq_2'=2,'dp'=8] {'seq_0','seq_1','seq_2','dp'}, use_global_device_ids=true, to_apply=%region_27.28 | all-reduce | flops 512 | bytes 4096 | tf_op jit(solution)/shard_map/psum | solution.py:143
  270.1 2.6 gather_fusion.1
  272.8 169.3 %all-reduce.3.cloned.1.call-done = (f32[512,1536]{1,0:T(8,128)}, f32[512,512]{1,0:T(8,128)}) async-done(((f32[512,1536]{1,0:T(8,128)}, f32[512,512]{1,0:T(8,128)}), (f32[512,1536]{1,0:T(8,128)}, f32[512,512]{1,0:T(8,128)})) %all-reduce.3.cloned.1.call-update) | async-done | bytes 4194320 | tf_op jit(solution)/shard_map/psum | solution.py:143
  442.1 3.8 copy.226
  445.9 1.0 copy.227
  (126 shorter events, 5.8 us)
Async XLA Ops:
  7.2 66.7 %copy-start = (bf16[512,1536]{1,0:T(8,128)(2,1)S(1)}, bf16[512,1536]{1,0:T(8,128)(2,1)}, u32[]{:S(2)}) copy-start(bf16[512,1536]{1,0:T(8,128)(2,1)} %param.9) | copy-start | bytes 4718596
  8.7 29.9 %copy-start.6 = (bf16[1,512,512]{2,1,0:T(8,128)(2,1)S(1)}, bf16[1,512,512]{2,1,0:T(8,128)(2,1)}, u32[]{:S(2)}) copy-start(bf16[1,512,512]{2,1,0:T(8,128)(2,1)} %param.7) | copy-start | bytes 1572868
  14.1 14.0 %all-to-all-start = ((s32[16,2,1,32]{3,1,2,0:T(2,128)}), s32[16,2,1,32]{3,1,2,0:T(2,128)S(1)}, u32[]{:S(2)}, u32[]{:S(2)}) async-start(s32[16,2,1,32]{3,1,2,0:T(2,128)} %bitcast.6), calls=%async_computation | async-start | bytes 32768 | tf_op jit(solution)/shard_map/all_to_all | solution.py:28
  34.9 20.2 %all-to-all-start.3 = ((bf16[16,2,1,32,512]{4,3,1,2,0:T(8,128)(2,1)}), bf16[16,2,1,32,512]{4,3,1,2,0:T(8,128)(2,1)S(1)}, u32[]{:S(2)}, u32[]{:S(2)}) async-start(bf16[16,2,1,32,512]{4,3,1,2,0:T(8,128)(2,1)} %bitcast.13), calls=%async_computation.3 | async-start | bytes 2097152 | tf_op jit(solution)/shard_map/all_to_all | solution.py:28
  42.9 24.4 %copy-start.29 = (s32[1024,1]{0,1:T(1,128)}, s32[1024,1]{0,1:T(1,128)S(1)}, u32[]{:S(2)}) copy-start(s32[1024,1]{0,1:T(1,128)S(1)} %get-tuple-element.26) | copy-start | bytes 12292
  61.6 34.7 %all-to-all-start.2 = ((bf16[32,32,512]{2,1,0:T(8,128)(2,1)}), bf16[32,32,512]{2,1,0:T(8,128)(2,1)}, u32[]{:S(2)}, u32[]{:S(2)}) async-start(bf16[32,32,512]{2,1,0:T(8,128)(2,1)} %bitcast.9), calls=%async_computation.2 | async-start | bytes 2097152 | tf_op jit(solution)/shard_map/all_to_all | solution.py:78
  66.2 7.7 %copy-start.26 = (f32[512]{0:T(512)S(1)}, f32[512]{0:T(512)}, u32[]{:S(2)}) copy-start(f32[512]{0:T(512)} %param.11) | copy-start | bytes 6148
  66.2 375.9 %all-reduce.3.cloned.1.call-start = ((), (), s32[]{:S(2)}) async-start(), calls=%async_computation.6 | async-start | bytes 8388608 | tf_op jit(solution)/shard_map/psum | solution.py:143
  79.6 10.9 %copy-start.13 = (bf16[512,128]{0,1:T(8,128)(2,1)}, bf16[512,128]{0,1:T(8,128)(2,1)S(1)}, u32[]{:S(2)}) copy-start(bf16[512,128]{0,1:T(8,128)(2,1)S(1)} %copy.172) | copy-start | bytes 393220
  79.9 6.7 %copy-start.16 = (bf16[512,128]{0,1:T(8,128)(2,1)}, bf16[512,128]{0,1:T(8,128)(2,1)S(1)}, u32[]{:S(2)}) copy-start(bf16[512,128]{0,1:T(8,128)(2,1)S(1)} %copy.169) | copy-start | bytes 393220
  80.0 6.6 %copy-start.18 = (bf16[512,128]{0,1:T(8,128)(2,1)}, bf16[512,128]{0,1:T(8,128)(2,1)S(1)}, u32[]{:S(2)}) copy-start(bf16[512,128]{0,1:T(8,128)(2,1)S(1)} %copy.168) | copy-start | bytes 393220
  80.1 4.2 copy-start.4
  80.3 4.1 copy-start.22
  80.4 4.0 copy-start.24
  82.6 1.8 copy-start.39
  86.6 1.8 copy-start.38
  86.6 1.8 copy-start.11
  90.5 1.8 copy-start.36
  90.5 1.8 copy-start.7
  90.5 1.8 copy-start.9
  94.5 1.8 copy-start.34
  94.5 7.6 %copy-start.3 = (bf16[512,512]{1,0:T(8,128)(2,1)S(1)}, bf16[512,512]{1,0:T(8,128)(2,1)}, u32[]{:S(2)}) copy-start(bf16[512,512]{1,0:T(8,128)(2,1)} %param.10) | copy-start | bytes 1572868
  102.1 0.9 copy-start.5
  107.6 5.0 %copy-start.25 = (bf16[512,128]{0,1:T(8,128)(2,1)S(1)}, bf16[512,128]{0,1:T(8,128)(2,1)}, u32[]{:S(2)}) copy-start(bf16[512,128]{0,1:T(8,128)(2,1)} %copy-done.24) | copy-start | bytes 393220
  117.7 1.8 copy-start.17
  121.6 5.1 %copy-start.19 = (bf16[512,128]{0,1:T(8,128)(2,1)S(1)}, bf16[512,128]{0,1:T(8,128)(2,1)}, u32[]{:S(2)}) copy-start(bf16[512,128]{0,1:T(8,128)(2,1)} %copy-done.18) | copy-start | bytes 393220
  131.8 1.8 copy-start.12
  131.8 1.8 copy-start.14
  135.5 4.9 %copy-start.37 = (f32[2,512]{1,0:T(2,128)S(1)}, f32[2,512]{1,0:T(2,128)}, u32[]{:S(2)}) copy-start(f32[2,512]{1,0:T(2,128)} %copy-done.36) | copy-start | bytes 12292
  145.5 1.8 copy-start.8
  145.5 1.8 copy-start.10
  145.5 1.8 copy-start.35
  153.5 5.1 %copy-start.23 = (bf16[2,64,512]{2,1,0:T(8,128)(2,1)S(1)}, bf16[2,64,512]{2,1,0:T(8,128)(2,1)}, u32[]{:S(2)}) copy-start(bf16[2,64,512]{2,1,0:T(8,128)(2,1)} %fusion.72) | copy-start | bytes 393220
  153.5 8.0 %copy-start.20 = (bf16[2,64,512]{2,1,0:T(8,128)(2,1)S(1)}, bf16[2,64,512]{2,1,0:T(8,128)(2,1)}, u32[]{:S(2)}) copy-start(bf16[2,64,512]{2,1,0:T(8,128)(2,1)} %fusion.75) | copy-start | bytes 393220
  153.5 8.0 %copy-start.21 = (bf16[2,64,512]{2,1,0:T(8,128)(2,1)S(1)}, bf16[2,64,512]{2,1,0:T(8,128)(2,1)}, u32[]{:S(2)}) copy-start(bf16[2,64,512]{2,1,0:T(8,128)(2,1)} %fusion.69) | copy-start | bytes 393220
  158.6 4.7 %copy-start.15 = (bf16[2,64,512]{2,1,0:T(8,128)(2,1)S(1)}, bf16[2,64,512]{2,1,0:T(8,128)(2,1)}, u32[]{:S(2)}) copy-start(bf16[2,64,512]{2,1,0:T(8,128)(2,1)} %convolution_convert_fusion.9) | copy-start | bytes 393220
  158.6 5.0 %copy-start.27 = (f32[512]{0:T(512)S(1)}, f32[512]{0:T(512)}, u32[]{:S(2)}) copy-start(f32[512]{0:T(512)} %param.11) | copy-start | bytes 6148
  163.6 2.8 copy-start.1
  163.6 2.8 copy-start.30
  163.6 2.8 copy-start.31
  163.7 2.7 copy-start.32
  163.7 2.7 copy-start.33
  167.8 0.7 copy-start.28
  176.8 93.3 %all-to-all-start.5 = ((bf16[32,32,512]{2,1,0:T(8,128)(2,1)}), bf16[32,32,512]{2,1,0:T(8,128)(2,1)S(1)}, u32[]{:S(2)}, u32[]{:S(2)}) async-start(bf16[32,32,512]{2,1,0:T(8,128)(2,1)} %bitcast.210), calls=%async_computation.5 | async-start | bytes 2097152 | tf_op jit(solution)/shard_map/all_to_all | solution.py:141
  442.1 3.8 copy-start.2
Sparse Core Ops, SparseCore 0:
  168.0 274.0 all-reduce.2
where the time goes:
time: 463 us; the launch traced here: 454 us
  waiting for transfers between devices  184 us (40%)
  blocking collectives  97.6 us (21%)
  matrix products  79.6 us (17%)
  local copies, waits for them, and re-layouts  48.7 us (11%)
  starting transfers between devices  23.4 us (5%)
  between operations  15 us (3%)
  other arithmetic  5.61 us (1%)
    psum x1, waiting for transfers between devices, per_device(): lax.psum((grad_qkv, grad_proj, gain_gradient), SEQ_DP)  169 us
    psum x1, blocking collectives, per_device(): lax.psum((grad_qkv, grad_proj, gain_gradient), SEQ_DP)  85.8 us
    dot_general x4, matrix products, per_device(): jnp.einsum('phqk,pkhd->pqhd', d_scores, keys, preferred_element_type=jnp....  20.5 us
    dot_general x4, matrix products, per_device(): jnp.einsum('phqk,pqhd->pkhd', d_scores, query, preferred_element_type=jnp...  19.9 us
    all_to_all x2, waiting for transfers between devices, turned_blocks(): lax.all_to_all(parts, axes[k], split_axis=k, concat_axis=k, tiled=True)  14.6 us
    scatter x4, local copies, waits for them, and re-layouts, unpack(): jnp.zeros((rows_dev, width), received.dtype).at[recv_flat]  12.3 us
    all_to_all x2, blocking collectives, turned_blocks(): lax.all_to_all(parts, axes[k], split_axis=k, concat_axis=k, tiled=True)  11.8 us
    all_to_all x2, starting transfers between devices, turned_blocks(): lax.all_to_all(parts, axes[k], split_axis=k, concat_axis=k, tiled=True)  11.2 us
  transfers between devices with their start and end apart: 5, of which 3 were waited for; matrix products, arithmetic and copies ran while one was open for 11% of the time, Pallas kernels for 0%

commit v1 on v0

v1 whole, which is shorter than its diff:
```python
import jax
import jax.numpy as jnp
from jax import lax
from jax.experimental import pallas as pl
from jax.experimental.pallas import tpu as pltpu
from jax.sharding import Mesh
from jax.sharding import PartitionSpec as P

SEQ = ("seq_0", "seq_1", "seq_2")
MESH_ID = pl.DeviceIdType.MESH
F32, BF16 = jnp.float32, jnp.bfloat16
ROWS = 512
C = 512
N_SEQ = 32
CAP = 32
SLOTS = N_SEQ * CAP
HEADS, HD = 8, 64
PAIRS = HEADS // 2
SCALE = 1.0 / HD**0.5
CHUNK = 2048


def nn(a, b):
    return jnp.dot(a, b, preferred_element_type=F32)


def nt(a, b):
    return lax.dot_general(a, b, (((1,), (1,)), ((), ())), preferred_element_type=F32)


def iota(shape, dim):
    return lax.broadcasted_iota(jnp.int32, shape, dim)


def hot(cond):
    return jnp.where(cond, 1.0, 0.0).astype(BF16)


def remote(src, dst, send, recv, device):
    return pltpu.make_async_remote_copy(
        src_ref=src, dst_ref=dst, send_sem=send, recv_sem=recv, device_id=device, device_id_type=MESH_ID
    )


def seq_peer(mx, my, mc, d, sign):
    dx, dy, dc = d // 8, (d // 2) % 4, d % 2
    return {
        "seq_0": lax.rem(mx + (dx if sign > 0 else 4 - dx), 4),
        "seq_1": lax.rem(my + (dy if sign > 0 else 4 - dy), 4),
        "seq_2": lax.rem(mc + dc, 2),
    }


def block_kernel(
    dest_ref, pts_ref, cot_ref, wqkv_ref, wproj_ref, gain_ref,
    out_ref, grads_ref, gg_ref,
    send_a, recv_a, send_b, recv_b, back, pos_send, pos_recv, pos_all,
    qkv, dattn, sgrad, xhat, invs, normed_t, dqkv, attn_t, probs, onehot_u, onehot_ut, onehot_pt,
    sem_send, sem_recv,
):
    mx, my, mc = lax.axis_index("seq_0"), lax.axis_index("seq_1"), lax.axis_index("seq_2")
    here = {"seq_0": mx, "seq_1": my, "seq_2": mc}
    barrier = pltpu.get_barrier_semaphore()
    for d in range(1, N_SEQ):
        pl.semaphore_signal(barrier, inc=1, device_id=seq_peer(mx, my, mc, d, 1), device_id_type=MESH_ID)

    dest = dest_ref[...]
    owner, slot = dest >> 9, dest & 511
    rel = ((((owner >> 3) - mx) & 3) << 3) | ((((owner >> 1) - my) & 3) << 1) | ((owner - mc) & 1)
    to_hot_f = jnp.where(iota((N_SEQ, ROWS), 0) == rel, 1.0, 0.0)
    to_hot = to_hot_f.astype(BF16)
    earlier = hot(iota((ROWS, ROWS), 0) < iota((ROWS, ROWS), 1))
    rank = jnp.sum(to_hot_f * nn(to_hot, earlier), axis=0, keepdims=True).astype(jnp.int32)
    sid = rel * CAP + rank
    rank_hot = hot(iota((128, ROWS), 0) == rank)
    pos_hi = nt((to_hot_f * (slot >> 4).astype(F32)).astype(BF16), rank_hot)
    pos_lo = nt((to_hot_f * (slot & 15).astype(F32)).astype(BF16), rank_hot)
    pos = pos_hi * 16.0 + pos_lo
    for d in range(N_SEQ):
        pos_send[d] = pos[d : d + 1, :]

    def pack(src_ref, send_ref, recv_ref):
        data = src_ref[...]

        def step(b, _):
            rows = pl.ds(pl.multiple_of(b * 256, 256), 256)
            pick = hot(iota((256, ROWS), 0) + b * 256 == sid)
            send_ref[rows, :] = nn(pick, data).astype(BF16)
            return 0

        lax.fori_loop(0, SLOTS // 256, step, 0)
        recv_ref[0:CAP, :] = send_ref[0:CAP, :]

    def send_all(send_ref, recv_ref, index, sign):
        for d in range(1, N_SEQ):
            rows = pl.ds(d * CAP, CAP)
            remote(send_ref.at[rows], recv_ref.at[rows], sem_send.at[index], sem_recv.at[index],
                   seq_peer(mx, my, mc, d, sign)).start()

    def wait_recv(ref, index):
        remote(ref, ref, sem_send.at[index], sem_recv.at[index], here).wait_recv()

    def wait_send(ref, index):
        remote(ref, ref, sem_send.at[index], sem_recv.at[index], here).wait_send()

    pack(pts_ref, send_a, recv_a)
    pl.semaphore_wait(barrier, N_SEQ - 1)
    for d in range(1, N_SEQ):
        remote(pos_send.at[d], pos_recv.at[d], sem_send.at[2], sem_recv.at[2],
               seq_peer(mx, my, mc, d, 1)).start()
    send_all(send_a, recv_a, 0, 1)
    pack(cot_ref, send_b, recv_b)
    send_all(send_b, recv_b, 1, 1)

    sid_col = jnp.transpose(jnp.broadcast_to(sid.astype(F32), (128, ROWS))).astype(jnp.int32)
    for j in range(SLOTS // 128):
        onehot_pt[:, j * 128 : (j + 1) * 128] = hot(iota((ROWS, 128), 1) + j * 128 == sid_col)

    others = pl.ds(CAP, SLOTS - CAP)
    wait_recv(pos_recv.at[pl.ds(1, N_SEQ - 1)], 2)
    pos_all[0:1, :] = pos_send[0]
    for d in range(1, N_SEQ):
        pos_all[d : d + 1, :] = pos_recv[d]
    got = pos_all[...].astype(jnp.int32)
    spread = hot(iota((128, SLOTS), 0) == (iota((128, SLOTS), 1) & 31))
    mine = iota((N_SEQ, SLOTS), 0) == (iota((N_SEQ, SLOTS), 1) >> 5)
    row_hi = nn((got >> 4).astype(F32).astype(BF16), spread)
    row_lo = nn((got & 15).astype(F32).astype(BF16), spread)
    row = jnp.sum(jnp.where(mine, row_hi * 16.0 + row_lo, 0.0), axis=0, keepdims=True).astype(jnp.int32)
    for j in range(ROWS // 128):
        onehot_u[j * 128 : (j + 1) * 128, :] = hot(iota((128, SLOTS), 0) + j * 128 == row)
    row_b = jnp.broadcast_to(row.astype(F32), (128, SLOTS))
    for j in range(SLOTS // 128):
        col = jnp.transpose(row_b[:, j * 128 : (j + 1) * 128]).astype(jnp.int32)
        for k in range(ROWS // 128):
            onehot_ut[j * 128 : (j + 1) * 128, k * 128 : (k + 1) * 128] = hot(iota((128, 128), 1) + k * 128 == col)

    wait_recv(recv_a.at[others], 0)
    serial = nn(onehot_u[...], recv_a[...])
    center = serial - jnp.mean(serial, axis=1, keepdims=True)
    inv = lax.rsqrt(jnp.mean(center * center, axis=1, keepdims=True) + 1e-05)
    standard = center * inv
    xhat[...] = standard
    invs[...] = jnp.broadcast_to(inv, (ROWS, 128))
    normed_f = (standard * gain_ref[...]).astype(BF16)
    normed_t[...] = jnp.transpose(normed_f)
    qkv[...] = nn(normed_f, wqkv_ref[...]).astype(BF16)

    low = iota((ROWS, 128), 1) < HD

    def cols(base, p):
        return pl.ds(pl.multiple_of(base + p * 128, 128), 128)

    def half(x, h):
        return jnp.where(low if h == 0 else ~low, x.astype(F32), 0.0)

    def forward(p, _):
        q, k, v = qkv[:, cols(0, p)], qkv[:, cols(C, p)], qkv[:, cols(2 * C, p)]
        v_t = jnp.transpose(v)
        for h in range(2):
            scores = nt((half(k, h) * SCALE).astype(BF16), q)
            expo = jnp.exp(scores - jnp.max(scores, axis=0, keepdims=True))
            prob = expo * (1.0 / jnp.sum(expo, axis=0, keepdims=True))
            probs[2 * p + h] = prob
            rows = pl.ds(pl.multiple_of(p * 128 + h * HD, HD), HD)
            attn_t[rows, :] = nn(v_t[h * HD : (h + 1) * HD], prob.astype(BF16)).astype(BF16)
        return 0

    lax.fori_loop(0, PAIRS, forward, 0)

    wait_recv(recv_b.at[others], 1)
    sgrad[...] = nn(onehot_u[...], recv_b[...]).astype(BF16)
    dattn[...] = nt(sgrad[...], wproj_ref[...]).astype(BF16)

    def backward(p, _):
        q, k, v = qkv[:, cols(0, p)], qkv[:, cols(C, p)], qkv[:, cols(2 * C, p)]
        d_a = dattn[:, cols(0, p)]
        k_t = jnp.transpose(k)
        dq_t, dk, dv = [], [], []
        for h in range(2):
            prob = probs[2 * p + h]
            d_prob = nt(half(v, h).astype(BF16), d_a)
            delta = jnp.sum(d_prob * prob, axis=0, keepdims=True)
            d_score = (prob * (d_prob - delta) * SCALE).astype(BF16)
            dq_t.append(nn(k_t[h * HD : (h + 1) * HD], d_score))
            dk.append(nn(d_score, q))
            dv.append(nn(prob.astype(BF16), d_a))
        dq = jnp.transpose(jnp.concatenate(dq_t, axis=0)).astype(BF16)
        dk = jnp.where(low, dk[0], dk[1]).astype(BF16)
        dv = jnp.where(low, dv[0], dv[1]).astype(BF16)
        for n, part in enumerate((dq, dk, dv)):
            dqkv[:, cols(n * C, p)] = part
            grads_ref[p, n * C : (n + 1) * C, :] = nn(normed_t[...], part)
        proj = nn(attn_t[pl.ds(pl.multiple_of(p * 128, 128), 128), :], sgrad[...])
        for j in range(4):
            grads_ref[p, 3 * C + j * 128 : 3 * C + (j + 1) * 128, :] = proj[:, j * 128 : (j + 1) * 128]
        return 0

    lax.fori_loop(0, PAIRS, backward, 0)

    d_normed = nt(dqkv[...], wqkv_ref[...])
    standard = xhat[...]
    gg = jnp.sum(d_normed * standard, axis=0, keepdims=True)
    for j in range(8):
        gg_ref[j : j + 1, :] = gg[:, j * 128 : (j + 1) * 128] if j < 4 else jnp.zeros((1, 128), F32)
    scaled = d_normed * gain_ref[...]
    first = jnp.mean(scaled, axis=1, keepdims=True)
    second = jnp.mean(scaled * standard, axis=1, keepdims=True)
    dx = (sgrad[...].astype(F32) + invs[:, 0:1] * (scaled - first - standard * second)).astype(BF16)
    wait_send(send_a.at[others], 0)
    send_a[...] = nn(onehot_ut[...], dx).astype(BF16)
    back[0:CAP, :] = send_a[0:CAP, :]
    send_all(send_a, back, 3, -1)
    wait_recv(back.at[others], 3)
    out_ref[...] = nn(onehot_pt[...], back[...]).astype(BF16)
    wait_send(pos_recv.at[pl.ds(1, N_SEQ - 1)], 2)
    wait_send(send_b.at[others], 1)
    wait_send(send_a.at[others], 3)


AXES = {"seq_0": 4, "seq_1": 4, "seq_2": 2, "dp": 8}


def reduce_kernel(
    grads_ref, gg_ref, out_ref, gg_out_ref,
    res, acc, acc2, acc3, core_buf, first_buf, second_buf, z_buf, g_core, g_x, g_y, g_z,
    sem_send, sem_recv, g_send, g_recv, out_sem,
):
    me = {a: lax.axis_index(a) for a in AXES}

    def peers(axis):
        n = AXES[axis]
        return [lax.rem(me[axis] + d, n) for d in range(1, n)]

    barrier = pltpu.get_barrier_semaphore()
    for axis in AXES:
        for t in peers(axis):
            pl.semaphore_signal(barrier, inc=1, device_id={axis: t}, device_id_type=MESH_ID)
    pl.semaphore_wait(barrier, sum(n - 1 for n in AXES.values()))

    def order(p):
        return ("seq_0", "seq_1") if p % 2 == 0 else ("seq_1", "seq_0")

    def rows(start, n):
        return pl.ds(pl.multiple_of(start, 8), n)

    def wait_recv(ref, stage, p):
        remote(ref, ref, sem_send.at[stage, p], sem_recv.at[stage, p], dict(me)).wait_recv()

    def wait_send(ref, stage, p):
        remote(ref, ref, sem_send.at[stage, p], sem_recv.at[stage, p], dict(me)).wait_send()

    def send(src, dst, stage, p, axis, t):
        remote(src, dst, sem_send.at[stage, p], sem_recv.at[stage, p], {axis: t}).start()

    core = me["seq_2"]
    half = CHUNK // 2
    for p in range(PAIRS):
        send(grads_ref.at[p, rows((1 - core) * half, half)], core_buf.at[p], 0, p, "seq_2", 1 - core)

    def gain_stage(k, axis, buf, value):
        m, n = me[axis], AXES[axis]
        buf[m] = value
        for t in peers(axis):
            remote(buf.at[m], buf.at[m], g_send.at[k], g_recv.at[k], {axis: t}).start()

    def gain_sum(k, axis, buf):
        n = AXES[axis]
        ref = buf.at[pl.ds(0, n - 1)]
        copy = remote(ref, ref, g_send.at[k], g_recv.at[k], dict(me))
        copy.wait_recv()
        copy.wait_send()
        total = buf[0]
        for j in range(1, n):
            total = total + buf[j]
        return total

    gain_stage(0, "seq_2", g_core, gg_ref[...])
    for p in range(PAIRS):
        first = order(p)[0]
        wait_recv(core_buf.at[p], 0, p)
        acc[p] = grads_ref[p, rows(core * half, half), :] + core_buf[p]
        for d, t in enumerate(peers(first)):
            send(acc.at[p, rows(t * 256, 256)], first_buf.at[p, d], 1, p, first, t)
    gain_stage(1, "seq_0", g_x, gain_sum(0, "seq_2", g_core))
    for p in range(PAIRS):
        first, second = order(p)
        wait_recv(first_buf.at[p], 1, p)
        acc2[p] = acc[p, rows(me[first] * 256, 256), :] + first_buf[p, 0] + first_buf[p, 1] + first_buf[p, 2]
        for d, t in enumerate(peers(second)):
            send(acc2.at[p, rows(t * 64, 64)], second_buf.at[p, d], 2, p, second, t)
    gain_stage(2, "seq_1", g_y, gain_sum(1, "seq_0", g_x))
    for p in range(PAIRS):
        first, second = order(p)
        wait_recv(second_buf.at[p], 2, p)
        acc3[p] = acc2[p, rows(me[second] * 64, 64), :] + second_buf[p, 0] + second_buf[p, 1] + second_buf[p, 2]
        for d, t in enumerate(peers("dp")):
            send(acc3.at[p, rows(t * 8, 8)], z_buf.at[p, d], 3, p, "dp", t)
    gain_stage(3, "dp", g_z, gain_sum(2, "seq_1", g_y))
    base1, base2, base3 = [], [], []
    for p in range(PAIRS):
        first, second = order(p)
        base1.append(core * half + me[first] * 256)
        base2.append(base1[p] + me[second] * 64)
        base3.append(base2[p] + me["dp"] * 8)
        wait_recv(z_buf.at[p], 3, p)
        total = acc3[p, rows(me["dp"] * 8, 8), :]
        for d in range(7):
            total = total + z_buf[p, d]
        own = rows(base3[p], 8)
        res[p, own, :] = total
        for t in peers("dp"):
            send(res.at[p, own], res.at[p, own], 4, p, "dp", t)
    for p in range(PAIRS):
        second = order(p)[1]
        wait_recv(res.at[p, pl.ds(0, 56)], 4, p)
        own = rows(base2[p], 64)
        for t in peers(second):
            send(res.at[p, own], res.at[p, own], 5, p, second, t)
    for p in range(PAIRS):
        first = order(p)[0]
        wait_recv(res.at[p, pl.ds(0, 192)], 5, p)
        own = rows(base1[p], 256)
        for t in peers(first):
            send(res.at[p, own], res.at[p, own], 6, p, first, t)
    for p in range(PAIRS):
        wait_recv(res.at[p, pl.ds(0, 768)], 6, p)
        own = rows(core * half, half)
        send(res.at[p, own], res.at[p, own], 7, p, "seq_2", 1 - core)
    gg_out_ref[...] = gain_sum(3, "dp", g_z)
    for p in range(PAIRS):
        wait_recv(res.at[p, pl.ds(0, half)], 7, p)
        pltpu.make_async_copy(res.at[p], out_ref.at[p], out_sem.at[p]).start()
    sent = (half, 768, 192, 56, 56, 192, 768, half)
    for p in range(PAIRS):
        for stage in range(8):
            wait_send(res.at[p, pl.ds(0, sent[stage])], stage, p)
        pltpu.make_async_copy(res.at[p], out_ref.at[p], out_sem.at[p]).wait()


def vmem(shape, dtype=F32):
    return pltpu.VMEM(shape, dtype)


DMA = pltpu.SemaphoreType.DMA
VSPEC = pl.BlockSpec(memory_space=pltpu.VMEM)


def per_device(points, cotangent, dest, w_qkv, w_proj, gain):
    big = lambda: vmem((SLOTS, C), BF16)
    grad_local, grads, gg = pl.pallas_call(
        block_kernel,
        name="block",
        out_shape=(
            jax.ShapeDtypeStruct((ROWS, C), BF16),
            jax.ShapeDtypeStruct((PAIRS, CHUNK, 128), F32),
            jax.ShapeDtypeStruct((8, 128), F32),
        ),
        in_specs=[VSPEC] * 6,
        out_specs=(VSPEC,) * 3,
        scratch_shapes=[
            big(), big(), big(), big(), big(),
            vmem((N_SEQ, 1, 128)), vmem((N_SEQ, 1, 128)), vmem((N_SEQ, 128)),
            vmem((ROWS, 3 * C), BF16), vmem((ROWS, C), BF16), vmem((ROWS, C), BF16),
            vmem((ROWS, C)), vmem((ROWS, 128)), vmem((C, ROWS), BF16), vmem((ROWS, 3 * C), BF16),
            vmem((C, ROWS), BF16), vmem((HEADS, ROWS, ROWS)),
            vmem((ROWS, SLOTS), BF16), vmem((SLOTS, ROWS), BF16), vmem((ROWS, SLOTS), BF16),
            DMA((4,)), DMA((4,)),
        ],
        compiler_params=pltpu.CompilerParams(
            collective_id=0, has_side_effects=True, vmem_limit_bytes=56 * 2**20
        ),
    )(dest, points[0], cotangent[0], w_qkv, w_proj, gain[None, :])
    reduced, gg = pl.pallas_call(
        reduce_kernel,
        name="reduce",
        out_shape=(
            jax.ShapeDtypeStruct((PAIRS, CHUNK, 128), F32),
            jax.ShapeDtypeStruct((8, 128), F32),
        ),
        in_specs=[VSPEC] * 2,
        out_specs=(pl.BlockSpec(memory_space=pl.ANY), VSPEC),
        scratch_shapes=[
            vmem((PAIRS, CHUNK, 128)), vmem((PAIRS, CHUNK // 2, 128)), vmem((PAIRS, 256, 128)),
            vmem((PAIRS, 64, 128)), vmem((PAIRS, CHUNK // 2, 128)), vmem((PAIRS, 3, 256, 128)),
            vmem((PAIRS, 3, 64, 128)), vmem((PAIRS, 7, 8, 128)),
            vmem((2, 8, 128)), vmem((4, 8, 128)), vmem((4, 8, 128)), vmem((8, 8, 128)),
            DMA((8, PAIRS)), DMA((8, PAIRS)), DMA((4,)), DMA((4,)), DMA((PAIRS,)),
        ],
        compiler_params=pltpu.CompilerParams(
            collective_id=1, has_side_effects=True, vmem_limit_bytes=56 * 2**20
        ),
    )(grads, gg)
    parts = reduced.reshape(PAIRS, 4, C, 128)
    grad_qkv = jnp.transpose(parts[:, :3], (2, 1, 0, 3)).reshape(C, 3 * C)
    proj = parts[:, 3].reshape(PAIRS, 4, 128, 128)
    grad_proj = jnp.transpose(proj, (0, 2, 1, 3)).reshape(C, C)
    return (grad_local[None], grad_qkv, grad_proj, gg[:4].reshape(C))


def solution(mesh):
    finer = Mesh(mesh.devices.reshape(4, 4, 2, mesh.shape["dp"]), ("seq_0", "seq_1", "seq_2", "dp"))
    placed = (P("dp", SEQ, None), P("dp", SEQ, None), P("dp", SEQ), P(), P(), P())
    return jax.shard_map(
        per_device,
        mesh=finer,
        in_specs=placed,
        out_specs=(P("dp", SEQ, None), P(), P(), P()),
        check_vma=False,
    )
```

time: 463 us -> 142 us (0.31); the launches traced: 454 us -> 141 us
  waiting for transfers between devices: 184 us -> 0 us
  Pallas kernels: 0 us -> 127 us
  blocking collectives: 97.6 us -> 0 us
  matrix products: 79.6 us -> 0 us
  local copies, waits for them, and re-layouts: 48.7 us -> 13.9 us
  starting transfers between devices: 23.4 us -> 0 us
  between operations: 15 us -> 0.67 us
  other arithmetic: 5.61 us -> 0 us
    psum x1 -> x0, waiting for transfers between devices: 169 us -> none  [per_device(): lax.psum((grad_qkv, grad_proj, gain_gradient), SEQ_DP)]
    pallas_call x0 -> x2, Pallas kernels: none -> 127 us  [the longest x1 64.7 us: per_device(): pl.pallas_call(block_kernel, name='block', out_shape=(jax.ShapeDtypeStruc...]
    psum x1 -> x0, blocking collectives: 85.8 us -> none  [per_device(): lax.psum((grad_qkv, grad_proj, gain_gradient), SEQ_DP)]
    dot_general x25 -> x0, matrix products: 70.9 us -> none  [the longest x4 20.5 us: per_device(): jnp.einsum('phqk,pkhd->pqhd', d_scores, keys, preferred_element_type=jnp....]
    all_to_all x4 -> x0, starting transfers between devices: 23.3 us -> none  [the longest x2 11.2 us: turned_blocks(): lax.all_to_all(parts, axes[k], split_axis=k, concat_axis=k, tiled=True)]
    scatter x7 -> x0, local copies, waits for them, and re-layouts: 22.2 us -> none  [the longest x4 12.3 us: unpack(): jnp.zeros((rows_dev, width), received.dtype).at[recv_flat]]
    all_to_all x4 -> x0, waiting for transfers between devices: 14.7 us -> none  [the longest x2 14.6 us: turned_blocks(): lax.all_to_all(parts, axes[k], split_axis=k, concat_axis=k, tiled=True)]
    all_to_all x2 -> x0, blocking collectives: 11.8 us -> none  [turned_blocks(): lax.all_to_all(parts, axes[k], split_axis=k, concat_axis=k, tiled=True)]
  transfers between devices with their start and end apart: 5 -> 0, of which waited for: 3 -> 0; matrix products, arithmetic and copies ran while one was open for 11% -> 0% of each run, Pallas kernels for 0% -> 0%
where the time goes in v1:
time: 142 us; the launch traced here: 141 us
  Pallas kernels  127 us (89%)
  local copies, waits for them, and re-layouts  13.9 us (10%)
    pallas_call x1, Pallas kernels, per_device(): pl.pallas_call(block_kernel, name='block', out_shape=(jax.ShapeDtypeStruc...  64.7 us
    pallas_call x1, Pallas kernels, per_device(): pl.pallas_call(reduce_kernel, name='reduce', out_shape=(jax.ShapeDtypeStr...  62.1 us
    transpose x2, local copies, waits for them, and re-layouts, per_device(): grad_qkv = jnp.transpose(parts[:, :3], (2, 1, 0, 3)).reshape(C, 3 * C)  4.12 us

profile of v1, /device:TPU:1, one launch (start us, length us, event | category | flops | bytes accessed | tf_op | source)
XLA Modules:
  0.0 141.4 jit_solution(15049343059304185417)
XLA Ops:
  0.6 64.7 %block.1 = (bf16[512,512]{1,0:T(8,128)(2,1)}, f32[4,2048,128]{2,1,0:T(8,128)}, f32[8,128]{1,0:T(8,128)}) custom-call(s32[1,512]{1,0:T(1,128)} %dest_ref.1, bf16[512,512]{1,0:T(8,128)(2,1)} %bitcast.22, bf16[512,512]{1,0:T(8,128)(2,1)} %bitcast.23, bf16[512,1536]{1,0:T(8,128)(2,1)} %wqkv_ref.1, bf16[512,512]{1,0:T(8,128)(2,1)} %wproj_ref.1, f32[1,512]{1,0:T(1,128)} %bitcast.24), custom_call_target="tpu_custom_call" | custom-call | tf_op jit(solution)/shard_map/block/pallas_call | solution.py:351
  65.4 62.1 %reduce.1 = (f32[4,2048,128]{2,1,0:T(8,128)}, f32[8,128]{1,0:T(8,128)}) custom-call(f32[4,2048,128]{2,1,0:T(8,128)} %get-tuple-element.10.grads_ref, f32[8,128]{1,0:T(8,128)} %get-tuple-element.11.gg_ref), custom_call_target="tpu_custom_call" | custom-call | tf_op jit(solution)/shard_map/reduce/pallas_call | solution.py:374
  127.5 1.3 slice_bitcast_fusion.1
  128.8 2.3 %slice.13 = f32[4,1,512,128]{3,2,1,0:T(8,128)} slice(f32[4,4,512,128]{3,2,1,0:T(8,128)} %bitcast.16), slice={[0:4], [3:4], [0:512], [0:128]} | slice | bytes 2097152 | tf_op jit(solution)/shard_map/slice | solution.py:396
  131.0 2.1 %slice_bitcast_fusion = f32[512,3,4,128]{3,0,1,2:T(8,128)S(1)} fusion(f32[4,4,512,128]{3,2,1,0:T(8,128)} %bitcast.17), kind=kLoop, calls=%fused_computation | loop fusion | bytes 6291456 | tf_op jit(solution)/shard_map/transpose | solution.py:395
  133.1 2.0 %copy.10 = f32[512,3,4,128]{3,2,1,0:T(4,128)S(1)} copy(f32[512,3,4,128]{3,0,1,2:T(8,128)S(1)} %slice_bitcast_fusion) | data formatting | bytes 6291456 | tf_op jit(solution)/shard_map/transpose | solution.py:395
  135.2 2.4 %reshape.21 = f32[512,1536]{1,0:T(8,128)} reshape(f32[512,3,4,128]{3,2,1,0:T(4,128)S(1)} %copy.10) | data formatting | bytes 6291456 | tf_op jit(solution)/shard_map/reshape | solution.py:395
  137.6 0.0 copy-start
  137.6 2.0 %copy.11 = f32[4,4,128,128]{3,1,2,0:T(4,128)S(1)} copy(f32[4,4,128,128]{3,2,1,0:T(8,128)} %bitcast.18) | data formatting | bytes 2097152 | tf_op jit(solution)/shard_map/reshape;squeeze | solution.py:396
  139.6 1.0 copy.14
  140.6 0.0 copy-done
  140.6 0.8 copy.16
Async XLA Ops:
  137.6 3.0 %copy-start = (bf16[512,512]{1,0:T(8,128)(2,1)S(1)}, bf16[512,512]{1,0:T(8,128)(2,1)}, u32[]{:S(2)}) copy-start(bf16[512,512]{1,0:T(8,128)(2,1)} %get-tuple-element.9) | copy-start | bytes 1572868
